TPU v7x, 256 devices: a whole 4x4x8 slice. The times are simulated.
256 devices in a mesh: gx: 16 (over y_hi, z), gy: 16 (over y_lo, x, core).
Axes of the slice: x: 4, y: 4 (y_hi: 2, y_lo: 2; y = y_hi * 2 + y_lo), z: 8, core: 2. Of those that a mesh axis runs over, the one named last changes fastest.
Arguments:
- inputs: bfloat16 [32, 64, 48, 128], P('gx', 'gy'), may hold values from -6 to 6
- cotangent: bfloat16 [32, 64, 48, 128], P('gx', 'gy'), may hold values from -6 to 6
- kernel: bfloat16 [27, 128, 128], replicated, may hold values from -0.109375 to 0.109375
Outputs:
- input_grad: bfloat16 [32, 64, 48, 128], P('gx', 'gy')
- kernel_grad: float32 [27, 128, 128], P(None, 'gx', 'gy')
All inputs are finite; a program needn't handle non-finite values.
Results may differ from a plain program's by a relative error of at most 0.0023.
Values may be sent and summed in bfloat16 or wider, within the bound.
A program may use at most 64 MiB of HBM per device.

v0:
```python
import math

import jax
import jax.numpy as jnp
from jax import lax
from jax.sharding import PartitionSpec as P


def padded_2(shard, sides, width):
    for axis, dim in sides:
        size, length = (lax.axis_size(axis), shard.shape[dim])
        up = [(i, (i + 1) % size) for i in range(size - 1)]
        down = [(j, i) for i, j in up]
        last = lax.slice_in_dim(shard, length - width, length, axis=dim)
        leading = lax.slice_in_dim(shard, 0, width, axis=dim)
        before = lax.ppermute(last, axis, up)
        after = lax.ppermute(leading, axis, down)
        shard = jnp.concatenate([before, shard, after], axis=dim)
    return shard


def in_blocks(shard, dim, length):
    before, after = (shard.shape[:dim], shard.shape[dim + 1 :])
    return jnp.moveaxis(shard.reshape(*before, length, -1, *after), dim, 0)


def sent_and_summed(shard, axis, dim):
    tiles = in_blocks(shard, dim, lax.axis_size(axis))
    arrived = lax.all_to_all(tiles, axis, split_axis=0, concat_axis=0, tiled=True)
    return arrived.sum(axis=0)


def depth_stack(padded, forward):
    depth = padded.shape[2]
    zpad = jnp.pad(padded, ((0, 0), (0, 0), (1, 1), (0, 0)))
    if forward:
        parts = [zpad[:, :, jz : jz + depth] for jz in range(3)]
    else:
        parts = [zpad[:, :, 2 - jz : 2 - jz + depth] for jz in range(3)]
    return jnp.concatenate(parts, axis=3)


def local(inputs, cotangent, kernel):
    widthx, widthy, depth, chans = inputs.shape
    values = inputs.astype(jnp.float32)
    normal_cdf = 0.5 * (1.0 + lax.erf(values / math.sqrt(2.0)))
    act = (values * normal_cdf).astype(jnp.bfloat16)
    slope = normal_cdf + values * jnp.exp(-0.5 * values * values) / math.sqrt(2.0 * math.pi)
    cot_flat = cotangent.reshape(-1, chans)
    both = padded_2(jnp.stack([act, cotangent]), (("gx", 1), ("gy", 2)), 1)
    act_stack = depth_stack(both[0], True)
    cot_stack = depth_stack(both[1], False)
    back = jnp.zeros((widthx * widthy * depth, chans), jnp.float32)
    grads = []
    for jx in range(3):
        for jy in range(3):
            first = jx * 9 + jy * 3
            weights = kernel[first : first + 3]
            gpiece = cot_stack[2 - jx : 2 - jx + widthx, 2 - jy : 2 - jy + widthy].reshape(
                -1, 3 * chans
            )
            stacked = jnp.transpose(weights, (0, 2, 1)).reshape(3 * chans, chans)
            back = back + jnp.dot(gpiece, stacked, preferred_element_type=jnp.float32)
            apiece = act_stack[jx : jx + widthx, jy : jy + widthy].reshape(-1, 3 * chans)
            term = lax.dot_general(
                apiece, cot_flat, (((0,), (0,)), ((), ())), preferred_element_type=jnp.float32
            )
            grads.append(term.reshape(3, chans, chans))
    input_grad = (slope * back.reshape(widthx, widthy, depth, chans)).astype(jnp.bfloat16)
    count_x = lax.axis_size("gx")
    count_y = lax.axis_size("gy")
    voxels = widthx * count_x * widthy * count_y * depth
    partial_grad = jnp.concatenate(grads, axis=0)
    rowsum = sent_and_summed(partial_grad, "gx", 1)
    summed = sent_and_summed(rowsum, "gy", 2)
    kernel_grad = summed / math.sqrt(voxels)
    return (input_grad, kernel_grad)


def solution(mesh):
    return jax.shard_map(
        local,
        mesh=mesh,
        in_specs=(P("gx", "gy", None, None), P("gx", "gy", None, None), P()),
        out_specs=(P("gx", "gy", None, None), P(None, "gx", "gy")),
        check_vma=False,
    )
```

profile of v0, /device:TPU:1, one launch (start us, length us, event | category | flops | bytes accessed | tf_op | source)
XLA Modules:
  0.0 105.0 jit_solution(16133902168988542709)
XLA Ops:
  0.6 0.9 fusion.10
  1.6 0.8 fusion.9
  2.4 1.3 %collective-permute-start.1 = (bf16[2,1,4,48,128]{4,3,2,1,0:T(8,128)(2,1)S(1)}, bf16[2,1,4,48,128]{4,3,2,1,0:T(8,128)(2,1)S(1)}, u32[]{:S(2)}, u32[]{:S(2)}) collective-permute-start(bf16[2,1,4,48,128]{4,3,2,1,0:T(8,128)(2,1)S(1)} %get-tuple-element.38), channel_id=1, source_target_pairs={{16,0},{32,16},{48,32},{64,48},{80,64},{96,80},{112,96},{128,112},... | collective-permute-start | bytes 294920 | tf_op jit(solution)/shard_map/ppermute | solution.py:17
  3.7 5.0 %collective-permute-start = (bf16[2,1,4,48,128]{4,3,2,1,0:T(8,128)(2,1)S(1)}, bf16[2,1,4,48,128]{4,3,2,1,0:T(8,128)(2,1)S(1)}, u32[]{:S(2)}, u32[]{:S(2)}) collective-permute-start(bf16[2,1,4,48,128]{4,3,2,1,0:T(8,128)(2,1)S(1)} %get-tuple-element.37), channel_id=1, source_target_pairs={{0,16},{16,32},{32,48},{48,64},{64,80},{80,96},{96,112},{112,128},... | collective-permute-start | bytes 294920 | tf_op jit(solution)/shard_map/ppermute | solution.py:16
  8.8 1.6 %collective-permute-done = bf16[2,1,4,48,128]{4,3,2,1,0:T(8,128)(2,1)S(1)} collective-permute-done((bf16[2,1,4,48,128]{4,3,2,1,0:T(8,128)(2,1)S(1)}, bf16[2,1,4,48,128]{4,3,2,1,0:T(8,128)(2,1)S(1)}, u32[]{:S(2)}, u32[]{:S(2)}) %collective-permute-start) | collective-permute-done | bytes 98336 | tf_op jit(solution)/shard_map/ppermute | solution.py:16
  10.4 0.8 pad_maximum_fusion.6
  11.1 5.3 %collective-permute-start.3 = (bf16[2,4,1,48,128]{4,3,2,1,0:T(8,128)(2,1)S(1)}, bf16[2,4,1,48,128]{4,3,2,1,0:T(8,128)(2,1)S(1)}, u32[]{:S(2)}, u32[]{:S(2)}) collective-permute-start(bf16[2,4,1,48,128]{4,3,2,1,0:T(8,128)(2,1)S(1)} %get-tuple-element.32), channel_id=1, source_target_pairs={{1,0},{2,1},{3,2},{4,3},{5,4},{6,5},{7,6},{8,7},{9,8},{10,9},{11,1... | collective-permute-start | bytes 294920 | tf_op jit(solution)/shard_map/ppermute | solution.py:17
  16.4 1.9 %collective-permute-start.2 = (bf16[2,4,1,48,128]{4,3,2,1,0:T(8,128)(2,1)S(1)}, bf16[2,4,1,48,128]{4,3,2,1,0:T(8,128)(2,1)S(1)}, u32[]{:S(2)}, u32[]{:S(2)}) collective-permute-start(bf16[2,4,1,48,128]{4,3,2,1,0:T(8,128)(2,1)S(1)} %get-tuple-element.31), channel_id=1, source_target_pairs={{0,1},{1,2},{2,3},{3,4},{4,5},{5,6},{6,7},{7,8},{8,9},{9,10},{10,1... | collective-permute-start | bytes 294920 | tf_op jit(solution)/shard_map/ppermute | solution.py:16
  18.4 1.6 %collective-permute-done.2 = bf16[2,4,1,48,128]{4,3,2,1,0:T(8,128)(2,1)S(1)} collective-permute-done((bf16[2,4,1,48,128]{4,3,2,1,0:T(8,128)(2,1)S(1)}, bf16[2,4,1,48,128]{4,3,2,1,0:T(8,128)(2,1)S(1)}, u32[]{:S(2)}, u32[]{:S(2)}) %collective-permute-start.2) | collective-permute-done | bytes 98336 | tf_op jit(solution)/shard_map/ppermute | solution.py:16
  20.0 1.0 pad_maximum_fusion.2
  21.6 1.1 %fusion.11 = (bf16[2,4,48,384]{3,2,1,0:T(8,128)(2,1)}, bf16[2,4,48,384]{3,2,1,0:T(8,128)(2,1)S(1)}, bf16[2,4,48,384]{3,2,1,0:T(8,128)(2,1)S(1)}, bf16[2,4,48,384...) fusion(bf16[4,6,48,384]{3,2,1,0:T(8,128)(2,1)S(1)} %get-tuple-e, ...), kind=kLoop, calls=%fused_computation.51 | loop fusion | bytes 5308416 | tf_op jit(solution)/shard_map/slice | solution.py:64
  22.7 1.2 %copy.41 = bf16[384,384]{0,1:T(8,128)(2,1)S(1)} copy(bf16[384,384]{1,0:T(8,128)(2,1)} %bitcast.171) | data formatting | bytes 589824 | tf_op jit(solution)/shard_map/reshape | solution.py:64
  23.8 0.9 copy.42
  26.1 1.2 %copy.49 = bf16[384,384]{0,1:T(8,128)(2,1)S(1)} copy(bf16[384,384]{1,0:T(8,128)(2,1)} %bitcast.162) | data formatting | bytes 589824 | tf_op jit(solution)/shard_map/reshape | solution.py:64
  27.5 1.2 %convolution_dynamic-update-slice_fusion.7 = f32[27,128,128]{2,1,0:T(8,128)S(1)} fusion(f32[27,128,128]{2,1,0:T(8,128)S(1)} %convolution_dynamic-update-slice_fusion.8, bf16[3,128,384]{2,1,0:T(8,128)(2,1)} %bitcast.153, bf16[384,128,1]{1,0,2:T(8,128)(2,1)S(1)} %bitcast.137), kind=kOutput, calls=%fused_computation.8 | convolution fusion | flops 37748736 | bytes 589824 | tf_op jit(solution)/shard_map/dot_general | solution.py:65
  30.4 1.3 %copy_bitcast_fusion = f32[16,27,8,128]{3,2,1,0:T(8,128)} fusion(f32[27,128,128]{2,1,0:T(8,128)S(1)} %convolution_dynamic-update-slice_fusion), kind=kLoop, calls=%fused_computation | loop fusion | bytes 3538944 | tf_op jit(solution)/shard_map/transpose | solution.py:24
  31.7 13.4 %all-to-all-start = ((f32[16,27,8,128]{3,2,1,0:T(8,128)}), f32[16,27,8,128]{3,2,1,0:T(8,128)S(1)}, u32[]{:S(2)}, u32[]{:S(2)}) async-start(f32[16,27,8,128]{3,2,1,0:T(8,128)} %copy_bitcast_fusion), calls=%async_computation | async-start | bytes 3538944 | tf_op jit(solution)/shard_map/all_to_all | solution.py:29
  45.2 0.9 fusion.12
  46.1 1.0 copy.55
  47.1 1.0 copy.56
  48.1 1.0 copy.57
  49.1 1.0 copy.58
  50.1 1.0 copy.59
  51.1 1.0 copy.60
  52.2 1.0 copy.61
  53.2 1.0 copy.62
  54.2 1.0 copy.63
  57.7 30.5 %all-to-all-done = f32[16,27,8,128]{3,2,1,0:T(8,128)S(1)} async-done(((f32[16,27,8,128]{3,2,1,0:T(8,128)}), f32[16,27,8,128]{3,2,1,0:T(8,128)S(1)}, u32[]{:S(2)}, u32[]{:S(2)}) %all-to-all-start) | async-done | bytes 1769504 | tf_op jit(solution)/shard_map/all_to_all | solution.py:29
  88.6 1.2 %reshape.147 = f32[16,1,1728]{2,1,0:T(1,128)} reshape(f32[16,8,8,27]{3,2,1,0:T(8,128)S(1)} %copy_bitcast_fusion.1) | data formatting | bytes 221184
  89.8 6.7 %all-to-all-start.1 = ((f32[16,1,1728]{2,1,0:T(1,128)}), f32[16,1,1728]{2,1,0:T(1,128)S(1)}, u32[]{:S(2)}, u32[]{:S(2)}) async-start(f32[16,1,1728]{2,1,0:T(1,128)} %reshape.147), calls=%async_computation.1 | async-start | bytes 229376 | tf_op jit(solution)/shard_map/all_to_all | solution.py:29
  97.2 5.2 %all-to-all-done.1 = f32[16,1,1728]{2,1,0:T(1,128)S(1)} async-done(((f32[16,1,1728]{2,1,0:T(1,128)}), f32[16,1,1728]{2,1,0:T(1,128)S(1)}, u32[]{:S(2)}, u32[]{:S(2)}) %all-to-all-start.1) | async-done | bytes 110624 | tf_op jit(solution)/shard_map/all_to_all | solution.py:29
  102.9 0.9 reduce
  (44 shorter events, 9.1 us)
Async XLA Ops:
  2.4 6.4 %collective-permute-start.1 = (bf16[2,1,4,48,128]{4,3,2,1,0:T(8,128)(2,1)S(1)}, bf16[2,1,4,48,128]{4,3,2,1,0:T(8,128)(2,1)S(1)}, u32[]{:S(2)}, u32[]{:S(2)}) collective-permute-start(bf16[2,1,4,48,128]{4,3,2,1,0:T(8,128)(2,1)S(1)} %get-tuple-element.38), channel_id=1, source_target_pairs={{16,0},{32,16},{48,32},{64,48},{80,64},{96,80},{112,96},{128,112},... | collective-permute-start | bytes 294920 | tf_op jit(solution)/shard_map/ppermute | solution.py:17
  3.7 6.6 %collective-permute-start = (bf16[2,1,4,48,128]{4,3,2,1,0:T(8,128)(2,1)S(1)}, bf16[2,1,4,48,128]{4,3,2,1,0:T(8,128)(2,1)S(1)}, u32[]{:S(2)}, u32[]{:S(2)}) collective-permute-start(bf16[2,1,4,48,128]{4,3,2,1,0:T(8,128)(2,1)S(1)} %get-tuple-element.37), channel_id=1, source_target_pairs={{0,16},{16,32},{32,48},{48,64},{64,80},{80,96},{96,112},{112,128},... | collective-permute-start | bytes 294920 | tf_op jit(solution)/shard_map/ppermute | solution.py:16
  11.1 7.2 %collective-permute-start.3 = (bf16[2,4,1,48,128]{4,3,2,1,0:T(8,128)(2,1)S(1)}, bf16[2,4,1,48,128]{4,3,2,1,0:T(8,128)(2,1)S(1)}, u32[]{:S(2)}, u32[]{:S(2)}) collective-permute-start(bf16[2,4,1,48,128]{4,3,2,1,0:T(8,128)(2,1)S(1)} %get-tuple-element.32), channel_id=1, source_target_pairs={{1,0},{2,1},{3,2},{4,3},{5,4},{6,5},{7,6},{8,7},{9,8},{10,9},{11,1... | collective-permute-start | bytes 294920 | tf_op jit(solution)/shard_map/ppermute | solution.py:17
  16.4 3.5 %collective-permute-start.2 = (bf16[2,4,1,48,128]{4,3,2,1,0:T(8,128)(2,1)S(1)}, bf16[2,4,1,48,128]{4,3,2,1,0:T(8,128)(2,1)S(1)}, u32[]{:S(2)}, u32[]{:S(2)}) collective-permute-start(bf16[2,4,1,48,128]{4,3,2,1,0:T(8,128)(2,1)S(1)} %get-tuple-element.31), channel_id=1, source_target_pairs={{0,1},{1,2},{2,3},{3,4},{4,5},{5,6},{6,7},{7,8},{8,9},{9,10},{10,1... | collective-permute-start | bytes 294920 | tf_op jit(solution)/shard_map/ppermute | solution.py:16
  24.9 2.3 %copy-start = (bf16[2,4,48,128]{3,2,1,0:T(8,128)(2,1)S(1)}, bf16[2,4,48,128]{3,2,1,0:T(8,128)(2,1)}, u32[]{:S(2)}) copy-start(bf16[2,4,48,128]{3,2,1,0:T(8,128)(2,1)} %param.4) | copy-start | bytes 294916
  31.7 13.4 %copy-start.1 = (bf16[27,128,128]{2,1,0:T(8,128)(2,1)S(1)}, bf16[27,128,128]{2,1,0:T(8,128)(2,1)}, u32[]{:S(2)}) copy-start(bf16[27,128,128]{2,1,0:T(8,128)(2,1)} %param.5) | copy-start | bytes 2654212
  31.7 56.5 %all-to-all-start = ((f32[16,27,8,128]{3,2,1,0:T(8,128)}), f32[16,27,8,128]{3,2,1,0:T(8,128)S(1)}, u32[]{:S(2)}, u32[]{:S(2)}) async-start(f32[16,27,8,128]{3,2,1,0:T(8,128)} %copy_bitcast_fusion), calls=%async_computation | async-start | bytes 3538944 | tf_op jit(solution)/shard_map/all_to_all | solution.py:29
  57.7 38.8 %copy-start.2 = (bf16[2,4,48,128]{3,2,1,0:T(8,128)(2,1)S(1)}, bf16[2,4,48,128]{3,2,1,0:T(8,128)(2,1)}, u32[]{:S(2)}) copy-start(bf16[2,4,48,128]{3,2,1,0:T(8,128)(2,1)} %param.3) | copy-start | bytes 294916
  89.8 12.6 %all-to-all-start.1 = ((f32[16,1,1728]{2,1,0:T(1,128)}), f32[16,1,1728]{2,1,0:T(1,128)S(1)}, u32[]{:S(2)}, u32[]{:S(2)}) async-start(f32[16,1,1728]{2,1,0:T(1,128)} %reshape.147), calls=%async_computation.1 | async-start | bytes 229376 | tf_op jit(solution)/shard_map/all_to_all | solution.py:29
where the time goes:
time: 106 us; the launch traced here: 105 us
  waiting for transfers between devices  38.9 us (37%)
  starting transfers between devices  33.6 us (32%)
  local copies, waits for them, and re-layouts  20.1 us (19%)
  other arithmetic  6.2 us (6%)
  matrix products  5.22 us (5%)
    all_to_all x2, waiting for transfers between devices, sent_and_summed(): lax.all_to_all(tiles, axis, split_axis=0, concat_axis=0, tiled=True)  35.7 us
    all_to_all x2, starting transfers between devices, sent_and_summed(): lax.all_to_all(tiles, axis, split_axis=0, concat_axis=0, tiled=True)  20.1 us
    unnamed x18, local copies, waits for them, and re-layouts  10.8 us
    ppermute x2, starting transfers between devices, padded_2(): before = lax.ppermute(last, axis, up)  6.93 us
    ppermute x2, starting transfers between devices, padded_2(): after = lax.ppermute(leading, axis, down)  6.56 us
    reshape x9, local copies, waits for them, and re-layouts, local(): apiece = act_stack[jx:jx + widthx, jy:jy + widthy].reshape(-1, 3 * chans)  4.55 us
    ppermute x2, waiting for transfers between devices, padded_2(): before = lax.ppermute(last, axis, up)  3.16 us
    dot_general x9, matrix products, local(): lax.dot_general(apiece, cot_flat, (((0,), (0,)), ((), ())), preferred_ele...  3.09 us
  transfers between devices with their start and end apart: 6, of which 5 were waited for; matrix products, arithmetic and copies ran while one was open for 13% of the time, Pallas kernels for 0%

commit v1 on v0

v1 whole, which is shorter than its diff:
```python
import math

import jax
import jax.numpy as jnp
from jax import lax
from jax.experimental import pallas as pl
from jax.experimental.pallas import tpu as pltpu
from jax.sharding import PartitionSpec as P

MESH = pl.DeviceIdType.MESH
F32 = jnp.float32
BF16 = jnp.bfloat16

WX, WY, DZ, C = 2, 4, 48, 128
VOX = WX * WY * DZ
NZ = 8
NQ = 8
NXY = 2 * NQ
PAIRS = 14
CHUNKS = (((0, 3), (0, 4)), ((3, 6), (4, 8)), ((6, 9), (8, 14)))
DIRS = tuple((dx, dy) for dx in (-1, 0, 1) for dy in (-1, 0, 1) if (dx, dy) != (0, 0))


def rim(d, width, send):
    if d == 0:
        return (1, width) if not send else (0, width)
    if send:
        return (width - 1, 1) if d > 0 else (0, 1)
    return (0, 1) if d > 0 else (width + 1, 1)


def body(
    inp_hbm, cot_hbm, ker_hbm, ig_ref, kg_ref,
    inp, wts, halo, stack, act_t, slope, acc, taps, parts, sib, xsend, xrecv, zsend, zrecv,
    load_sem, hsend_sem, hrecv_sem, ssend_sem, srecv_sem, xsend_sem, xrecv_sem, zsend_sem, zrecv_sem,
):
    gx, gy = lax.axis_index("gx"), lax.axis_index("gy")
    core, q = gy % 2, gy // 2
    z, yh = gx % NZ, gx // NZ
    here = yh * NQ + q
    other = gy + 1 - 2 * core

    def xy_peer(m):
        return ((m // NQ) * NZ + z, (m % NQ) * 2 + core)

    def z_peer(k):
        return (yh * NZ + k, gy)

    barrier = pltpu.get_barrier_semaphore()

    def greet(dev):
        pl.semaphore_signal(barrier, inc=1, device_id=dev, device_id_type=MESH)

    for dx, dy in DIRS:
        greet(((gx + dx + 16) % 16, (gy + dy + 16) % 16))
    greet((gx, other))

    @pl.loop(1, NXY)
    def _(d):
        greet(xy_peer((here + d) % NXY))

    @pl.loop(1, NZ)
    def _(d):
        greet(z_peer((z + d) % NZ))

    own = halo.at[pl.ds(1, WX), pl.ds(1, WY)]
    load_cot = pltpu.make_async_copy(cot_hbm, own, load_sem.at[0])
    load_inp = pltpu.make_async_copy(inp_hbm, inp, load_sem.at[1])
    load_ker = pltpu.make_async_copy(ker_hbm, wts, load_sem.at[2])
    load_cot.start()
    load_inp.start()
    load_ker.start()

    def has(d, at, size):
        if d == 0:
            return 1
        return jnp.where(at < size - 1, 1, 0) if d > 0 else jnp.where(at > 0, 1, 0)

    def hop(i):
        dx, dy = DIRS[i]
        sx, sy = rim(dx, WX, True), rim(dy, WY, True)
        lx, ly = rim(dx, WX, False), rim(dy, WY, False)
        return pltpu.make_async_remote_copy(
            src_ref=cot_hbm.at[pl.ds(*sx), pl.ds(*sy)],
            dst_ref=halo.at[pl.ds(*lx), pl.ds(*ly)],
            send_sem=hsend_sem.at[i],
            recv_sem=hrecv_sem.at[i],
            device_id=((gx + dx + 16) % 16, (gy + dy + 16) % 16),
            device_id_type=MESH,
        )

    pl.semaphore_wait(barrier, len(DIRS) + 1 + (NXY - 1) + (NZ - 1))

    for i, (dx, dy) in enumerate(DIRS):
        @pl.when(has(dx, gx, 16) * has(dy, gy, 16) == 1)
        def _():
            hop(i).start()

    for i, (dx, dy) in enumerate(DIRS):
        lx, ly = rim(dx, WX, False), rim(dy, WY, False)

        @pl.when(has(-dx, gx, 16) * has(-dy, gy, 16) == 0)
        def _():
            halo[pl.ds(*lx), pl.ds(*ly)] = jnp.zeros((lx[1], ly[1], DZ, C), BF16)

    load_inp.wait()

    @pl.loop(0, WX)
    def _(x):
        v = inp[x].astype(F32).reshape(WY * DZ, C)
        cdf = 0.5 * (1.0 + lax.erf(v / math.sqrt(2.0)))
        slope[x] = cdf + v * jnp.exp(-0.5 * v * v) / math.sqrt(2.0 * math.pi)
        act = (v * cdf).astype(BF16)
        act_t[x] = act.astype(F32).T.astype(BF16)

    row = lax.broadcasted_iota(jnp.int32, (DZ, C), 0)

    def restack(x, y):
        v = halo[x, y].astype(F32)
        up = jnp.where(row == DZ - 1, 0.0, pltpu.roll(v, DZ - 1, 0))
        down = jnp.where(row == 0, 0.0, pltpu.roll(v, 1, 0))
        stack[x, y] = jnp.concatenate([up, v, down], axis=1).astype(BF16)

    load_cot.wait()

    @pl.loop(0, WX * WY)
    def _(k):
        restack(1 + k // WY, 1 + k % WY)

    taps[27] = jnp.zeros((C, C), F32)
    load_ker.wait()

    for i, (dx, dy) in enumerate(DIRS):
        @pl.when(has(-dx, gx, 16) * has(-dy, gy, 16) == 1)
        def _():
            hop(i).wait_recv()

    @pl.loop(0, WY + 2)
    def _(y):
        restack(0, y)
        restack(WX + 1, y)

    @pl.loop(0, WX)
    def _(x):
        restack(1 + x, 0)
        restack(1 + x, WY + 1)

    def window(w):
        jx, jy = w // 3, w % 3
        return stack[pl.ds(2 - jx, WX), pl.ds(2 - jy, WY)].reshape(VOX, 3 * C)

    def sib_copy(k):
        lo, hi = CHUNKS[k][1]
        return pltpu.make_async_remote_copy(
            src_ref=parts.at[1 - core, pl.ds(lo, hi - lo)],
            dst_ref=sib.at[pl.ds(lo, hi - lo)],
            send_sem=ssend_sem.at[k],
            recv_sem=srecv_sem.at[k],
            device_id=(gx, other),
            device_id_type=MESH,
        )

    def xy_copy(k, d, arriving=False):
        lo, hi = CHUNKS[k][1][0] // 2, CHUNKS[k][1][1] // 2
        to = (here + d) % NXY
        slot = (here + NXY - d) % NXY if arriving else here
        return pltpu.make_async_remote_copy(
            src_ref=xsend.at[to, pl.ds(lo, hi - lo)],
            dst_ref=xrecv.at[slot, pl.ds(lo, hi - lo)],
            send_sem=xsend_sem.at[k, d],
            recv_sem=xrecv_sem.at[k, d],
            device_id=xy_peer(to),
            device_id_type=MESH,
        )

    def z_copy(d, arriving=False):
        to = (z + d) % NZ
        slot = (z + NZ - d) % NZ if arriving else z
        return pltpu.make_async_remote_copy(
            src_ref=zsend.at[to],
            dst_ref=zrecv.at[slot],
            send_sem=zsend_sem.at[d],
            recv_sem=zrecv_sem.at[d],
            device_id=z_peer(to),
            device_id_type=MESH,
        )

    lhs = jnp.concatenate([act_t[x] for x in range(WX)], axis=1)

    def compute(k):
        (w_lo, w_hi), (lo, hi) = CHUNKS[k]

        @pl.loop(w_lo, w_hi)
        def _(w):
            r = jnp.dot(lhs, window(w), preferred_element_type=F32)
            for jz in range(3):
                taps[3 * w + jz] = r[:, jz * C : (jz + 1) * C]

        @pl.loop(lo, hi)
        def _(u):
            for h in range(2):
                a = jnp.concatenate(
                    [taps[2 * u, 64 * h : 64 * h + 64], taps[2 * u + 1, 64 * h : 64 * h + 64]], axis=0
                )
                t = a.T.reshape(NQ, 2, 8, C)
                parts[0, u, h] = t[:, 0]
                parts[1, u, h] = t[:, 1]

        sib_copy(k).start()

    def forward(k):
        lo, hi = CHUNKS[k][1]
        sib_copy(k).wait_recv()

        @pl.loop(lo // 2, hi // 2)
        def _(v):
            for h in range(2):
                both = [parts[core, 2 * v + e, h] + sib[2 * v + e, h] for e in range(2)]
                xsend[NQ * h : NQ * h + NQ, v] = jnp.concatenate(both, axis=1).astype(BF16)

        @pl.loop(1, NXY)
        def _(d):
            xy_copy(k, d).start()

    compute(0)
    compute(1)
    forward(0)
    compute(2)
    forward(1)
    forward(2)

    acc[...] = jnp.zeros_like(acc)

    @pl.loop(0, 9)
    def _(w):
        wt = jnp.concatenate([wts[3 * w + jz] for jz in range(3)], axis=1)
        acc[...] += lax.dot_general(
            window(w), wt, (((1,), (1,)), ((), ())), preferred_element_type=F32
        )

    for x in range(WX):
        back = acc[pl.ds(x * WY * DZ, WY * DZ)]
        ig_ref[x] = (slope[x] * back).astype(BF16).reshape(WY, DZ, C)

    for k in range(len(CHUNKS)):
        @pl.loop(1, NXY)
        def _(d):
            xy_copy(k, d, arriving=True).wait_recv()

    xrecv[here] = xsend[here]
    total = xrecv[0].astype(F32)
    for m in range(1, NXY):
        total = total + xrecv[m].astype(F32)
    total = jnp.concatenate([total.reshape(8 * PAIRS, C), jnp.zeros((C - 8 * PAIRS, C), F32)], axis=0)
    turned = total.T.reshape(2, NZ, 8, C)
    for e in range(2):
        zsend[:, e] = turned[e]

    @pl.loop(1, NZ)
    def _(d):
        z_copy(d).start()

    zrecv[z] = zsend[z]

    @pl.loop(1, NZ)
    def _(d):
        z_copy(d, arriving=True).wait_recv()

    out = zrecv[0]
    for m in range(1, NZ):
        out = out + zrecv[m]
    kg_ref[...] = out

    for i, (dx, dy) in enumerate(DIRS):
        @pl.when(has(dx, gx, 16) * has(dy, gy, 16) == 1)
        def _():
            hop(i).wait_send()

    for k in range(len(CHUNKS)):
        sib_copy(k).wait_send()

        @pl.loop(1, NXY)
        def _(d):
            xy_copy(k, d).wait_send()

    @pl.loop(1, NZ)
    def _(d):
        z_copy(d).wait_send()


def local(inputs, cotangent, kernel):
    n = len(CHUNKS)
    hbm = pl.BlockSpec(memory_space=pl.ANY)
    vmem = pl.BlockSpec(memory_space=pltpu.VMEM)
    dma = pltpu.SemaphoreType.DMA
    input_grad, sums = pl.pallas_call(
        body,
        out_shape=(
            jax.ShapeDtypeStruct((WX, WY, DZ, C), BF16),
            jax.ShapeDtypeStruct((2, 8, C), F32),
        ),
        in_specs=[hbm, hbm, hbm],
        out_specs=(vmem, vmem),
        scratch_shapes=[
            pltpu.VMEM((WX, WY, DZ, C), BF16),
            pltpu.VMEM((27, C, C), BF16),
            pltpu.VMEM((WX + 2, WY + 2, DZ, C), BF16),
            pltpu.VMEM((WX + 2, WY + 2, DZ, 3 * C), BF16),
            pltpu.VMEM((WX, C, WY * DZ), BF16),
            pltpu.VMEM((WX, WY * DZ, C), F32),
            pltpu.VMEM((VOX, C), F32),
            pltpu.VMEM((28, C, C), F32),
            pltpu.VMEM((2, PAIRS, 2, NQ, 8, C), F32),
            pltpu.VMEM((PAIRS, 2, NQ, 8, C), F32),
            pltpu.VMEM((NXY, PAIRS // 2, 16, C), BF16),
            pltpu.VMEM((NXY, PAIRS // 2, 16, C), BF16),
            pltpu.VMEM((NZ, 2, 8, C), F32),
            pltpu.VMEM((NZ, 2, 8, C), F32),
            dma((3,)),
            dma((8,)),
            dma((8,)),
            dma((n,)),
            dma((n,)),
            dma((n, NXY)),
            dma((n, NXY)),
            dma((NZ,)),
            dma((NZ,)),
        ],
        compiler_params=pltpu.CompilerParams(
            collective_id=0, has_side_effects=True, vmem_limit_bytes=32 * 1024 * 1024
        ),
        name="conv_backward",
    )(*(pltpu.with_memory_space_constraint(a, pltpu.HBM) for a in (inputs, cotangent, kernel)))
    voxels = 32 * 64 * 48
    grad = sums.reshape(2, 8, 16, 8).transpose(2, 0, 1, 3).reshape(32, 8, 8)[:27]
    return (input_grad, grad / math.sqrt(voxels))


def solution(mesh):
    return jax.shard_map(
        local,
        mesh=mesh,
        in_specs=(P("gx", "gy", None, None), P("gx", "gy", None, None), P()),
        out_specs=(P("gx", "gy", None, None), P(None, "gx", "gy")),
        check_vma=False,
    )
```

time: 106 us -> 34 us (0.32)
  waiting for transfers between devices: 38.9 us -> 0 us
  starting transfers between devices: 33.6 us -> 0 us
  Pallas kernels: 0 us -> 31.7 us
  local copies, waits for them, and re-layouts: 20.1 us -> 1.52 us
  other arithmetic: 6.2 us -> 0.01 us
  matrix products: 5.22 us -> 0 us
    all_to_all x2 -> x0, waiting for transfers between devices: 35.7 us -> none  [sent_and_summed(): lax.all_to_all(tiles, axis, split_axis=0, concat_axis=0, tiled=True)]
    pallas_call x0 -> x1, Pallas kernels: none -> 31.7 us  [local(): pl.pallas_call(body, out_shape=(jax.ShapeDtypeStruct((WX, WY, DZ, C), BF1...]
    all_to_all x2 -> x0, starting transfers between devices: 20.1 us -> none  [sent_and_summed(): lax.all_to_all(tiles, axis, split_axis=0, concat_axis=0, tiled=True)]
    ppermute x4 -> x0, starting transfers between devices: 13.5 us -> none  [the longest x2 6.93 us: padded_2(): before = lax.ppermute(last, axis, up)]
    unnamed x18 -> x2, local copies, waits for them, and re-layouts: 10.8 us -> 1.38 us
    dot_general x18 -> x0, matrix products: 5.22 us -> none  [the longest x9 3.09 us: local(): lax.dot_general(apiece, cot_flat, (((0,), (0,)), ((), ())), preferred_ele...]
    reshape x9 -> x1, local copies, waits for them, and re-layouts: 4.55 us -> 0.1 us  [local(): sums.reshape(2, 8, 16, 8).transpose(2, 0, 1, 3).reshape(32, 8, 8)[:27]]
    ppermute x4 -> x0, waiting for transfers between devices: 3.23 us -> none  [the longest x2 3.16 us: padded_2(): before = lax.ppermute(last, axis, up)]
  transfers between devices with their start and end apart: 6 -> 0, of which waited for: 5 -> 0; matrix products, arithmetic and copies ran while one was open for 13% -> 0% of each run, Pallas kernels for 0% -> 0%
where the time goes in v1:
time: 34 us; the launch traced here: 33.9 us
  Pallas kernels  31.7 us (93%)
  local copies, waits for them, and re-layouts  1.52 us (4%)
  between operations  0.66 us (2%)
    pallas_call x1, Pallas kernels, local(): pl.pallas_call(body, out_shape=(jax.ShapeDtypeStruct((WX, WY, DZ, C), BF1...  31.7 us
    unnamed x2, local copies, waits for them, and re-layouts  1.38 us

profile of v1, /device:TPU:1, one launch (start us, length us, event | category | flops | bytes accessed | tf_op | source)
XLA Modules:
  0.0 33.9 jit_solution(12492150099904516570)
XLA Ops:
  0.6 31.7 %conv_backward.1 = (bf16[2,4,48,128]{3,2,1,0:T(8,128)(2,1)S(1)}, f32[2,8,128]{2,1,0:T(8,128)S(1)}) custom-call(bf16[2,4,48,128]{3,2,1,0:T(8,128)(2,1)} %inp_hbm.1, bf16[2,4,48,128]{3,2,1,0:T(8,128)(2,1)} %cot_hbm.1, bf16[27,128,128]{2,1,0:T(8,128)(2,1)} %ker_hbm.1), custom_call_target="tpu_custom_call" | custom-call | tf_op jit(solution)/shard_map/conv_backward/pallas_call | solution.py:296
  32.4 0.1 reshape.10
  32.5 0.7 %copy.7 = f32[27,8,8]{0,2,1:T(8,128)} copy(f32[27,8,8]{2,1,0:T(8,128)S(1)} %slice_multiply_fusion) | data formatting | bytes 13824
  33.3 0.6 %copy.9 = bf16[2,4,48,128]{3,2,1,0:T(8,128)(2,1)} copy(bf16[2,4,48,128]{3,2,1,0:T(8,128)(2,1)S(1)} %get-tuple-element.10) | data formatting | bytes 196608
  (2 shorter events, 0.1 us)

commit v2 on v1

--- a/solution.py
+++ b/solution.py
@@ -17,8 +17,20 @@
 NQ = 8
 NXY = 2 * NQ
 PAIRS = 14
+ORDER = (3, 4, 5, 0, 1, 2, 6, 7, 8)
 CHUNKS = (((0, 3), (0, 4)), ((3, 6), (4, 8)), ((6, 9), (8, 14)))
 DIRS = tuple((dx, dy) for dx in (-1, 0, 1) for dy in (-1, 0, 1) if (dx, dy) != (0, 0))
+
+
+def blocks(w, local):
+    jx, jy = w // 3, w % 3
+    every = [(x, y) for x in range(WX) for y in range(WY)]
+    inside = [(x, y) for x, y in every if 1 <= x + 2 - jx <= WX and 1 <= y + 2 - jy <= WY]
+    return inside if local else [b for b in every if b not in inside]
+
+
+LOCAL = [blocks(w, True) for w in range(9)]
+RIM = [blocks(w, False) for w in range(9)]
 
 
 def rim(d, width, send):
@@ -31,7 +43,7 @@
 
 def body(
     inp_hbm, cot_hbm, ker_hbm, ig_ref, kg_ref,
-    inp, wts, halo, stack, act_t, slope, acc, taps, parts, sib, xsend, xrecv, zsend, zrecv,
+    inp, wts, halo, stack, act, slope, acc, taps, parts, sib, xsend, xrecv, zsend, zrecv, sums,
     load_sem, hsend_sem, hrecv_sem, ssend_sem, srecv_sem, xsend_sem, xrecv_sem, zsend_sem, zrecv_sem,
 ):
     gx, gy = lax.axis_index("gx"), lax.axis_index("gy")
@@ -110,8 +122,7 @@
         v = inp[x].astype(F32).reshape(WY * DZ, C)
         cdf = 0.5 * (1.0 + lax.erf(v / math.sqrt(2.0)))
         slope[x] = cdf + v * jnp.exp(-0.5 * v * v) / math.sqrt(2.0 * math.pi)
-        act = (v * cdf).astype(BF16)
-        act_t[x] = act.astype(F32).T.astype(BF16)
+        act[x] = (v * cdf).astype(BF16).astype(F32).reshape(WY, DZ, C)
 
     row = lax.broadcasted_iota(jnp.int32, (DZ, C), 0)
 
@@ -127,23 +138,34 @@
     def _(k):
         restack(1 + k // WY, 1 + k % WY)
 
+    def gather(lhs_blocks):
+        return jnp.concatenate([act[x, y] for x, y in lhs_blocks], axis=0).T.astype(BF16)
+
+    def product(w, chosen):
+        jx, jy = w // 3, w % 3
+        rows = [stack[x + 2 - jx, y + 2 - jy] for x, y in chosen]
+        return jnp.dot(lhs[w, chosen is RIM[w]], jnp.concatenate(rows, axis=0), preferred_element_type=F32)
+
+    lhs = {}
+    for w in ORDER:
+        lhs[w, False] = gather(LOCAL[w])
+        if RIM[w]:
+            lhs[w, True] = gather(RIM[w])
+    for n, w in enumerate(ORDER):
+        r = product(w, LOCAL[w])
+        for jz in range(3):
+            taps[3 * n + jz] = r[:, jz * C : (jz + 1) * C]
     taps[27] = jnp.zeros((C, C), F32)
     load_ker.wait()
 
-    for i, (dx, dy) in enumerate(DIRS):
-        @pl.when(has(-dx, gx, 16) * has(-dy, gy, 16) == 1)
-        def _():
-            hop(i).wait_recv()
-
-    @pl.loop(0, WY + 2)
-    def _(y):
-        restack(0, y)
-        restack(WX + 1, y)
-
-    @pl.loop(0, WX)
-    def _(x):
-        restack(1 + x, 0)
-        restack(1 + x, WY + 1)
+    def landed(along_x):
+        for i, (dx, dy) in enumerate(DIRS):
+            if (dx != 0) != along_x:
+                continue
+
+            @pl.when(has(-dx, gx, 16) * has(-dy, gy, 16) == 1)
+            def _():
+                hop(i).wait_recv()
 
     def window(w):
         jx, jy = w // 3, w % 3
@@ -185,16 +207,14 @@
             device_id_type=MESH,
         )
 
-    lhs = jnp.concatenate([act_t[x] for x in range(WX)], axis=1)
-
     def compute(k):
         (w_lo, w_hi), (lo, hi) = CHUNKS[k]
-
-        @pl.loop(w_lo, w_hi)
-        def _(w):
-            r = jnp.dot(lhs, window(w), preferred_element_type=F32)
-            for jz in range(3):
-                taps[3 * w + jz] = r[:, jz * C : (jz + 1) * C]
+        for n in range(w_lo, w_hi):
+            w = ORDER[n]
+            if RIM[w]:
+                r = product(w, RIM[w])
+                for jz in range(3):
+                    taps[3 * n + jz] += r[:, jz * C : (jz + 1) * C]
 
         @pl.loop(lo, hi)
         def _(u):
@@ -222,7 +242,21 @@
         def _(d):
             xy_copy(k, d).start()
 
+    landed(False)
+
+    @pl.loop(0, WX)
+    def _(x):
+        restack(1 + x, 0)
+        restack(1 + x, WY + 1)
+
     compute(0)
+    landed(True)
+
+    @pl.loop(0, WY + 2)
+    def _(y):
+        restack(0, y)
+        restack(WX + 1, y)
+
     compute(1)
     forward(0)
     compute(2)
@@ -251,7 +285,9 @@
     total = xrecv[0].astype(F32)
     for m in range(1, NXY):
         total = total + xrecv[m].astype(F32)
-    total = jnp.concatenate([total.reshape(8 * PAIRS, C), jnp.zeros((C - 8 * PAIRS, C), F32)], axis=0)
+    sums[pl.ds(0, 8 * PAIRS)] = total.reshape(8 * PAIRS, C)
+    sums[pl.ds(8 * PAIRS, C - 8 * PAIRS)] = jnp.zeros((C - 8 * PAIRS, C), F32)
+    total = jnp.concatenate([sums[pl.ds(o, 16, stride=8)] for o in range(8)], axis=0)
     turned = total.T.reshape(2, NZ, 8, C)
     for e in range(2):
         zsend[:, e] = turned[e]
@@ -286,6 +322,22 @@
     @pl.loop(1, NZ)
     def _(d):
         z_copy(d).wait_send()
+
+
+def finish(ig_ref, sums_ref, out_ref, grad_ref, turn):
+    out_ref[...] = ig_ref[...]
+    total = sums_ref[...].reshape(16, C) / math.sqrt(32 * 64 * 48)
+    for o in range(8):
+        turn[pl.ds(o, 16, stride=8)] = pltpu.roll(total, (C - 16 * o) % C, 1)
+    pair = turn[...].reshape(2, 8, 8, C)
+    lane = lax.broadcasted_iota(jnp.int32, (8, C), 1)
+    block = lane // 9
+    place = lane + jnp.where(block == 0, 9, jnp.where(block == 1, -9, 0))
+    source = jnp.minimum(place // 2, 15)
+    for i in range(8):
+        even = jnp.take_along_axis(pair[0, i], source, axis=1)
+        odd = jnp.take_along_axis(pair[1, i], source, axis=1)
+        grad_ref[i] = jnp.where(place % 2 == 0, even, odd)[:, :27]
 
 
 def local(inputs, cotangent, kernel):
@@ -306,7 +358,7 @@
             pltpu.VMEM((27, C, C), BF16),
             pltpu.VMEM((WX + 2, WY + 2, DZ, C), BF16),
             pltpu.VMEM((WX + 2, WY + 2, DZ, 3 * C), BF16),
-            pltpu.VMEM((WX, C, WY * DZ), BF16),
+            pltpu.VMEM((WX, WY, DZ, C), F32),
             pltpu.VMEM((WX, WY * DZ, C), F32),
             pltpu.VMEM((VOX, C), F32),
             pltpu.VMEM((28, C, C), F32),
@@ -316,6 +368,7 @@
             pltpu.VMEM((NXY, PAIRS // 2, 16, C), BF16),
             pltpu.VMEM((NZ, 2, 8, C), F32),
             pltpu.VMEM((NZ, 2, 8, C), F32),
+            pltpu.VMEM((C, C), F32),
             dma((3,)),
             dma((8,)),
             dma((8,)),
@@ -331,9 +384,20 @@
         ),
         name="conv_backward",
     )(*(pltpu.with_memory_space_constraint(a, pltpu.HBM) for a in (inputs, cotangent, kernel)))
-    voxels = 32 * 64 * 48
-    grad = sums.reshape(2, 8, 16, 8).transpose(2, 0, 1, 3).reshape(32, 8, 8)[:27]
-    return (input_grad, grad / math.sqrt(voxels))
+    whole = lambda shape: pl.BlockSpec(shape, lambda: (0,) * len(shape))
+    input_grad, grad = pl.pallas_call(
+        finish,
+        out_shape=(
+            jax.ShapeDtypeStruct((WX, WY, DZ, C), BF16),
+            jax.ShapeDtypeStruct((8, 8, 27), F32),
+        ),
+        in_specs=[vmem, vmem],
+        out_specs=(whole((WX, WY, DZ, C)), whole((8, 8, 27))),
+        scratch_shapes=[pltpu.VMEM((C, C), F32)],
+        compiler_params=pltpu.CompilerParams(vmem_limit_bytes=2 * 1024 * 1024),
+        name="finish",
+    )(input_grad, sums)
+    return (input_grad, grad.transpose(2, 0, 1))
 
 
 def solution(mesh):

time: 34 us -> 31.7 us (0.932)
  local copies, waits for them, and re-layouts: 1.52 us -> 0 us
  Pallas kernels: 31.7 us -> 31 us
    pallas_call x1, Pallas kernels: 31.7 us -> 30.2 us  [local(): pl.pallas_call(body, out_shape=(jax.ShapeDtypeStruct((WX, WY, DZ, C), BF1...]
    unnamed x2 -> x0, local copies, waits for them, and re-layouts: 1.38 us -> none
    pallas_call x0 -> x1, Pallas kernels: none -> 0.79 us  [local(): pl.pallas_call(finish, out_shape=(jax.ShapeDtypeStruct((WX, WY, DZ, C), B...]
where the time goes in v2:
time: 31.7 us; the launch traced here: 31.6 us
  Pallas kernels  31 us (98%)
  between operations  0.64 us (2%)
    pallas_call x1, Pallas kernels, local(): pl.pallas_call(body, out_shape=(jax.ShapeDtypeStruct((WX, WY, DZ, C), BF1...  30.2 us
    pallas_call x1, Pallas kernels, local(): pl.pallas_call(finish, out_shape=(jax.ShapeDtypeStruct((WX, WY, DZ, C), B...  0.79 us

profile of v2, /device:TPU:1, one launch (start us, length us, event | category | flops | bytes accessed | tf_op | source)
XLA Modules:
  0.0 31.6 jit_solution(17437282380601156301)
XLA Ops:
  0.6 30.2 %conv_backward.1 = (bf16[2,4,48,128]{3,2,1,0:T(8,128)(2,1)S(1)}, f32[2,8,128]{2,1,0:T(8,128)S(1)}) custom-call(bf16[2,4,48,128]{3,2,1,0:T(8,128)(2,1)} %inp_hbm.1, bf16[2,4,48,128]{3,2,1,0:T(8,128)(2,1)} %cot_hbm.1, bf16[27,128,128]{2,1,0:T(8,128)(2,1)} %ker_hbm.1), custom_call_target="tpu_custom_call" | custom-call | tf_op jit(solution)/shard_map/conv_backward/pallas_call | solution.py:348
  30.8 0.8 %finish.1 = (bf16[2,4,48,128]{3,2,1,0:T(8,128)(2,1)}, f32[8,8,27]{2,1,0:T(8,128)}) custom-call(bf16[2,4,48,128]{3,2,1,0:T(8,128)(2,1)S(1)} %get-tuple-element.6.ig_ref, f32[2,8,128]{2,1,0:T(8,128)S(1)} %get-tuple-element.7.sums_ref), custom_call_target="tpu_custom_call" | custom-call | tf_op jit(solution)/shard_map/finish/pallas_call | solution.py:388

commit v3 on v2

--- a/solution.py
+++ b/solution.py
@@ -17,8 +17,20 @@
 NQ = 8
 NXY = 2 * NQ
 PAIRS = 14
-ORDER = (3, 4, 5, 0, 1, 2, 6, 7, 8)
-CHUNKS = (((0, 3), (0, 4)), ((3, 6), (4, 8)), ((6, 9), (8, 14)))
+ORDER = (4, 3, 5, 0, 1, 2, 6, 7, 8)
+CHUNKS = (((0, 1), (0, 1)), ((1, 3), (1, 2)), ((3, 6), (2, 4)), ((6, 9), (4, 7)))
+STEPS = ('c0', 'f0', 'y', 'c1', 'x', 'c2', 'f1', 'c3', 'f2', 'f3')
+
+
+def slot(n, jz):
+    return 3 * n + jz + (1 if n else 0)
+
+
+XY = sorted(
+    ((dx, dy) for dx in range(4) for dy in range(4) if dx or dy),
+    key=lambda d: -(min(d[0], 4 - d[0]) + min(d[1], 4 - d[1])),
+)
+ZS = (4, 3, 5, 2, 6, 1, 7)
 DIRS = tuple((dx, dy) for dx in (-1, 0, 1) for dy in (-1, 0, 1) if (dx, dy) != (0, 0))
 
 
@@ -50,10 +62,13 @@
     core, q = gy % 2, gy // 2
     z, yh = gx % NZ, gx // NZ
     here = yh * NQ + q
+    px, py = q % 4, yh * 2 + q // 4
     other = gy + 1 - 2 * core
 
-    def xy_peer(m):
-        return ((m // NQ) * NZ + z, (m % NQ) * 2 + core)
+    def xy_peer(d):
+        x, y = (px + d[0]) % 4, (py + d[1]) % 4
+        m = y * 4 + x
+        return m, ((m // NQ) * NZ + z, (m % NQ) * 2 + core)
 
     def z_peer(k):
         return (yh * NZ + k, gy)
@@ -63,17 +78,13 @@
     def greet(dev):
         pl.semaphore_signal(barrier, inc=1, device_id=dev, device_id_type=MESH)
 
+    for d in XY:
+        greet(xy_peer(d)[1])
+    for d in ZS:
+        greet(z_peer((z + d) % NZ))
     for dx, dy in DIRS:
         greet(((gx + dx + 16) % 16, (gy + dy + 16) % 16))
     greet((gx, other))
-
-    @pl.loop(1, NXY)
-    def _(d):
-        greet(xy_peer((here + d) % NXY))
-
-    @pl.loop(1, NZ)
-    def _(d):
-        greet(z_peer((z + d) % NZ))
 
     own = halo.at[pl.ds(1, WX), pl.ds(1, WY)]
     load_cot = pltpu.make_async_copy(cot_hbm, own, load_sem.at[0])
@@ -154,10 +165,8 @@
     for n, w in enumerate(ORDER):
         r = product(w, LOCAL[w])
         for jz in range(3):
-            taps[3 * n + jz] = r[:, jz * C : (jz + 1) * C]
-    taps[27] = jnp.zeros((C, C), F32)
-    load_ker.wait()
-
+            taps[slot(n, jz)] = r[:, jz * C : (jz + 1) * C]
+    taps[3] = jnp.zeros((C, C), F32)
     def landed(along_x):
         for i, (dx, dy) in enumerate(DIRS):
             if (dx != 0) != along_x:
@@ -174,38 +183,56 @@
     def sib_copy(k):
         lo, hi = CHUNKS[k][1]
         return pltpu.make_async_remote_copy(
-            src_ref=parts.at[1 - core, pl.ds(lo, hi - lo)],
-            dst_ref=sib.at[pl.ds(lo, hi - lo)],
+            src_ref=parts.at[1 - core, pl.ds(2 * lo, 2 * (hi - lo))],
+            dst_ref=sib.at[pl.ds(2 * lo, 2 * (hi - lo))],
             send_sem=ssend_sem.at[k],
             recv_sem=srecv_sem.at[k],
             device_id=(gx, other),
             device_id_type=MESH,
         )
 
-    def xy_copy(k, d, arriving=False):
-        lo, hi = CHUNKS[k][1][0] // 2, CHUNKS[k][1][1] // 2
-        to = (here + d) % NXY
-        slot = (here + NXY - d) % NXY if arriving else here
+    def xy_copy(k, d):
+        lo, hi = CHUNKS[k][1]
+        m, twin = xy_peer(d)
         return pltpu.make_async_remote_copy(
-            src_ref=xsend.at[to, pl.ds(lo, hi - lo)],
-            dst_ref=xrecv.at[slot, pl.ds(lo, hi - lo)],
-            send_sem=xsend_sem.at[k, d],
-            recv_sem=xrecv_sem.at[k, d],
-            device_id=xy_peer(to),
+            src_ref=xsend.at[m, pl.ds(lo, hi - lo)],
+            dst_ref=xrecv.at[here, pl.ds(lo, hi - lo)],
+            send_sem=xsend_sem.at[k],
+            recv_sem=xrecv_sem.at[k],
+            device_id=twin,
             device_id_type=MESH,
         )
 
-    def z_copy(d, arriving=False):
+    def xy_all(k):
+        lo, hi = CHUNKS[k][1]
+        return pltpu.make_async_remote_copy(
+            src_ref=xsend.at[pl.ds(0, NXY - 1), pl.ds(lo, hi - lo)],
+            dst_ref=xrecv.at[pl.ds(0, NXY - 1), pl.ds(lo, hi - lo)],
+            send_sem=xsend_sem.at[k],
+            recv_sem=xrecv_sem.at[k],
+            device_id=(gx, other),
+            device_id_type=MESH,
+        )
+
+    def z_copy(d):
         to = (z + d) % NZ
-        slot = (z + NZ - d) % NZ if arriving else z
         return pltpu.make_async_remote_copy(
             src_ref=zsend.at[to],
-            dst_ref=zrecv.at[slot],
-            send_sem=zsend_sem.at[d],
-            recv_sem=zrecv_sem.at[d],
+            dst_ref=zrecv.at[z],
+            send_sem=zsend_sem,
+            recv_sem=zrecv_sem,
             device_id=z_peer(to),
             device_id_type=MESH,
         )
+
+    z_all = pltpu.make_async_remote_copy(
+        src_ref=zsend.at[pl.ds(0, NZ - 1)],
+        dst_ref=zrecv.at[pl.ds(0, NZ - 1)],
+        send_sem=zsend_sem,
+        recv_sem=zrecv_sem,
+        device_id=(gx, other),
+        device_id_type=MESH,
+    )
 
     def compute(k):
         (w_lo, w_hi), (lo, hi) = CHUNKS[k]
@@ -214,9 +241,9 @@
             if RIM[w]:
                 r = product(w, RIM[w])
                 for jz in range(3):
-                    taps[3 * n + jz] += r[:, jz * C : (jz + 1) * C]
-
-        @pl.loop(lo, hi)
+                    taps[slot(n, jz)] += r[:, jz * C : (jz + 1) * C]
+
+        @pl.loop(2 * lo, 2 * hi)
         def _(u):
             for h in range(2):
                 a = jnp.concatenate(
@@ -232,37 +259,36 @@
         lo, hi = CHUNKS[k][1]
         sib_copy(k).wait_recv()
 
-        @pl.loop(lo // 2, hi // 2)
+        @pl.loop(lo, hi)
         def _(v):
             for h in range(2):
                 both = [parts[core, 2 * v + e, h] + sib[2 * v + e, h] for e in range(2)]
                 xsend[NQ * h : NQ * h + NQ, v] = jnp.concatenate(both, axis=1).astype(BF16)
 
-        @pl.loop(1, NXY)
-        def _(d):
+        for d in XY:
             xy_copy(k, d).start()
 
-    landed(False)
-
-    @pl.loop(0, WX)
-    def _(x):
-        restack(1 + x, 0)
-        restack(1 + x, WY + 1)
-
-    compute(0)
-    landed(True)
-
-    @pl.loop(0, WY + 2)
-    def _(y):
-        restack(0, y)
-        restack(WX + 1, y)
-
-    compute(1)
-    forward(0)
-    compute(2)
-    forward(1)
-    forward(2)
-
+    for step in STEPS:
+        if step == "y":
+            landed(False)
+
+            @pl.loop(0, WX)
+            def _(x):
+                restack(1 + x, 0)
+                restack(1 + x, WY + 1)
+        elif step == "x":
+            landed(True)
+
+            @pl.loop(0, WY + 2)
+            def _(y):
+                restack(0, y)
+                restack(WX + 1, y)
+        elif step[0] == "c":
+            compute(int(step[1]))
+        else:
+            forward(int(step[1]))
+
+    load_ker.wait()
     acc[...] = jnp.zeros_like(acc)
 
     @pl.loop(0, 9)
@@ -277,9 +303,7 @@
         ig_ref[x] = (slope[x] * back).astype(BF16).reshape(WY, DZ, C)
 
     for k in range(len(CHUNKS)):
-        @pl.loop(1, NXY)
-        def _(d):
-            xy_copy(k, d, arriving=True).wait_recv()
+        xy_all(k).wait_recv()
 
     xrecv[here] = xsend[here]
     total = xrecv[0].astype(F32)
@@ -292,36 +316,25 @@
     for e in range(2):
         zsend[:, e] = turned[e]
 
-    @pl.loop(1, NZ)
-    def _(d):
+    for d in ZS:
         z_copy(d).start()
-
     zrecv[z] = zsend[z]
 
-    @pl.loop(1, NZ)
-    def _(d):
-        z_copy(d, arriving=True).wait_recv()
-
+    for i, (dx, dy) in enumerate(DIRS):
+        @pl.when(has(dx, gx, 16) * has(dy, gy, 16) == 1)
+        def _():
+            hop(i).wait_send()
+
+    for k in range(len(CHUNKS)):
+        sib_copy(k).wait_send()
+        xy_all(k).wait_send()
+
+    z_all.wait_recv()
     out = zrecv[0]
     for m in range(1, NZ):
         out = out + zrecv[m]
     kg_ref[...] = out
-
-    for i, (dx, dy) in enumerate(DIRS):
-        @pl.when(has(dx, gx, 16) * has(dy, gy, 16) == 1)
-        def _():
-            hop(i).wait_send()
-
-    for k in range(len(CHUNKS)):
-        sib_copy(k).wait_send()
-
-        @pl.loop(1, NXY)
-        def _(d):
-            xy_copy(k, d).wait_send()
-
-    @pl.loop(1, NZ)
-    def _(d):
-        z_copy(d).wait_send()
+    z_all.wait_send()
 
 
 def finish(ig_ref, sums_ref, out_ref, grad_ref, turn):
@@ -331,8 +344,9 @@
         turn[pl.ds(o, 16, stride=8)] = pltpu.roll(total, (C - 16 * o) % C, 1)
     pair = turn[...].reshape(2, 8, 8, C)
     lane = lax.broadcasted_iota(jnp.int32, (8, C), 1)
-    block = lane // 9
-    place = lane + jnp.where(block == 0, 9, jnp.where(block == 1, -9, 0))
+    place = lane
+    for n, w in enumerate(ORDER):
+        place = jnp.where(lane // 3 == w, lane - 3 * w + slot(n, 0), place)
     source = jnp.minimum(place // 2, 15)
     for i in range(8):
         even = jnp.take_along_axis(pair[0, i], source, axis=1)
@@ -374,10 +388,10 @@
             dma((8,)),
             dma((n,)),
             dma((n,)),
-            dma((n, NXY)),
-            dma((n, NXY)),
-            dma((NZ,)),
-            dma((NZ,)),
+            dma((n,)),
+            dma((n,)),
+            dma,
+            dma,
         ],
         compiler_params=pltpu.CompilerParams(
             collective_id=0, has_side_effects=True, vmem_limit_bytes=32 * 1024 * 1024

time: 31.7 us -> 29.8 us (0.940)
  Pallas kernels: 31 us -> 29.1 us
    pallas_call x1, Pallas kernels: 30.2 us -> 28.3 us  [local(): pl.pallas_call(body, out_shape=(jax.ShapeDtypeStruct((WX, WY, DZ, C), BF1...]
where the time goes in v3:
time: 29.8 us; the launch traced here: 29.7 us
  Pallas kernels  29.1 us (98%)
  between operations  0.64 us (2%)
    pallas_call x1, Pallas kernels, local(): pl.pallas_call(body, out_shape=(jax.ShapeDtypeStruct((WX, WY, DZ, C), BF1...  28.3 us
    pallas_call x1, Pallas kernels, local(): pl.pallas_call(finish, out_shape=(jax.ShapeDtypeStruct((WX, WY, DZ, C), B...  0.79 us

profile of v3, /device:TPU:1, one launch (start us, length us, event | category | flops | bytes accessed | tf_op | source)
XLA Modules:
  0.0 29.7 jit_solution(12051773108408512772)
XLA Ops:
  0.6 28.3 %conv_backward.1 = (bf16[2,4,48,128]{3,2,1,0:T(8,128)(2,1)S(1)}, f32[2,8,128]{2,1,0:T(8,128)S(1)}) custom-call(bf16[2,4,48,128]{3,2,1,0:T(8,128)(2,1)} %inp_hbm.1, bf16[2,4,48,128]{3,2,1,0:T(8,128)(2,1)} %cot_hbm.1, bf16[27,128,128]{2,1,0:T(8,128)(2,1)} %ker_hbm.1), custom_call_target="tpu_custom_call" | custom-call | tf_op jit(solution)/shard_map/conv_backward/pallas_call | solution.py:362
  28.9 0.8 %finish.1 = (bf16[2,4,48,128]{3,2,1,0:T(8,128)(2,1)}, f32[8,8,27]{2,1,0:T(8,128)}) custom-call(bf16[2,4,48,128]{3,2,1,0:T(8,128)(2,1)S(1)} %get-tuple-element.6.ig_ref, f32[2,8,128]{2,1,0:T(8,128)S(1)} %get-tuple-element.7.sums_ref), custom_call_target="tpu_custom_call" | custom-call | tf_op jit(solution)/shard_map/finish/pallas_call | solution.py:402

commit v4 on v3

--- a/solution.py
+++ b/solution.py
@@ -31,6 +31,9 @@
     key=lambda d: -(min(d[0], 4 - d[0]) + min(d[1], 4 - d[1])),
 )
 ZS = (4, 3, 5, 2, 6, 1, 7)
+ROW = ((2, 0), (1, 0), (3, 0))
+COLUMN = ((0, 2), (0, 1), (0, 3))
+NEAR_Z = (2, 6, 1, 7)
 DIRS = tuple((dx, dy) for dx in (-1, 0, 1) for dy in (-1, 0, 1) if (dx, dy) != (0, 0))
 
 
@@ -57,6 +60,7 @@
     inp_hbm, cot_hbm, ker_hbm, ig_ref, kg_ref,
     inp, wts, halo, stack, act, slope, acc, taps, parts, sib, xsend, xrecv, zsend, zrecv, sums,
     load_sem, hsend_sem, hrecv_sem, ssend_sem, srecv_sem, xsend_sem, xrecv_sem, zsend_sem, zrecv_sem,
+    plane_in, z_in,
 ):
     gx, gy = lax.axis_index("gx"), lax.axis_index("gy")
     core, q = gy % 2, gy // 2
@@ -78,13 +82,12 @@
     def greet(dev):
         pl.semaphore_signal(barrier, inc=1, device_id=dev, device_id_type=MESH)
 
-    for d in XY:
-        greet(xy_peer(d)[1])
-    for d in ZS:
-        greet(z_peer((z + d) % NZ))
     for dx, dy in DIRS:
         greet(((gx + dx + 16) % 16, (gy + dy + 16) % 16))
-    greet((gx, other))
+    for d in (*ROW, *COLUMN):
+        greet(xy_peer(d)[1])
+    for d in NEAR_Z:
+        greet(z_peer((z + d) % NZ))
 
     own = halo.at[pl.ds(1, WX), pl.ds(1, WY)]
     load_cot = pltpu.make_async_copy(cot_hbm, own, load_sem.at[0])
@@ -104,27 +107,13 @@
         sx, sy = rim(dx, WX, True), rim(dy, WY, True)
         lx, ly = rim(dx, WX, False), rim(dy, WY, False)
         return pltpu.make_async_remote_copy(
-            src_ref=cot_hbm.at[pl.ds(*sx), pl.ds(*sy)],
+            src_ref=halo.at[pl.ds(1 + sx[0], sx[1]), pl.ds(1 + sy[0], sy[1])],
             dst_ref=halo.at[pl.ds(*lx), pl.ds(*ly)],
             send_sem=hsend_sem.at[i],
             recv_sem=hrecv_sem.at[i],
             device_id=((gx + dx + 16) % 16, (gy + dy + 16) % 16),
             device_id_type=MESH,
         )
-
-    pl.semaphore_wait(barrier, len(DIRS) + 1 + (NXY - 1) + (NZ - 1))
-
-    for i, (dx, dy) in enumerate(DIRS):
-        @pl.when(has(dx, gx, 16) * has(dy, gy, 16) == 1)
-        def _():
-            hop(i).start()
-
-    for i, (dx, dy) in enumerate(DIRS):
-        lx, ly = rim(dx, WX, False), rim(dy, WY, False)
-
-        @pl.when(has(-dx, gx, 16) * has(-dy, gy, 16) == 0)
-        def _():
-            halo[pl.ds(*lx), pl.ds(*ly)] = jnp.zeros((lx[1], ly[1], DZ, C), BF16)
 
     load_inp.wait()
 
@@ -167,6 +156,26 @@
         for jz in range(3):
             taps[slot(n, jz)] = r[:, jz * C : (jz + 1) * C]
     taps[3] = jnp.zeros((C, C), F32)
+    pl.semaphore_wait(barrier, len(DIRS) + len(ROW) + len(COLUMN) + len(NEAR_Z))
+
+    for i, (dx, dy) in enumerate(DIRS):
+        @pl.when(has(dx, gx, 16) * has(dy, gy, 16) == 1)
+        def _():
+            hop(i).start()
+
+    for d in ROW:
+        pl.semaphore_signal(plane_in, inc=1, device_id=xy_peer(d)[1], device_id_type=MESH)
+    for d in NEAR_Z:
+        pl.semaphore_signal(z_in, inc=1, device_id=z_peer((z + d) % NZ), device_id_type=MESH)
+
+
+    for i, (dx, dy) in enumerate(DIRS):
+        lx, ly = rim(dx, WX, False), rim(dy, WY, False)
+
+        @pl.when(has(-dx, gx, 16) * has(-dy, gy, 16) == 0)
+        def _():
+            halo[pl.ds(*lx), pl.ds(*ly)] = jnp.zeros((lx[1], ly[1], DZ, C), BF16)
+
     def landed(along_x):
         for i, (dx, dy) in enumerate(DIRS):
             if (dx != 0) != along_x:
@@ -243,8 +252,7 @@
                 for jz in range(3):
                     taps[slot(n, jz)] += r[:, jz * C : (jz + 1) * C]
 
-        @pl.loop(2 * lo, 2 * hi)
-        def _(u):
+        for u in range(2 * lo, 2 * hi):
             for h in range(2):
                 a = jnp.concatenate(
                     [taps[2 * u, 64 * h : 64 * h + 64], taps[2 * u + 1, 64 * h : 64 * h + 64]], axis=0
@@ -265,6 +273,8 @@
                 both = [parts[core, 2 * v + e, h] + sib[2 * v + e, h] for e in range(2)]
                 xsend[NQ * h : NQ * h + NQ, v] = jnp.concatenate(both, axis=1).astype(BF16)
 
+        if k == 0:
+            pl.semaphore_wait(plane_in, len(ROW))
         for d in XY:
             xy_copy(k, d).start()
 
@@ -272,15 +282,13 @@
         if step == "y":
             landed(False)
 
-            @pl.loop(0, WX)
-            def _(x):
+            for x in range(WX):
                 restack(1 + x, 0)
                 restack(1 + x, WY + 1)
         elif step == "x":
             landed(True)
 
-            @pl.loop(0, WY + 2)
-            def _(y):
+            for y in range(WY + 2):
                 restack(0, y)
                 restack(WX + 1, y)
         elif step[0] == "c":
@@ -316,6 +324,7 @@
     for e in range(2):
         zsend[:, e] = turned[e]
 
+    pl.semaphore_wait(z_in, len(NEAR_Z))
     for d in ZS:
         z_copy(d).start()
     zrecv[z] = zsend[z]
@@ -392,6 +401,8 @@
             dma((n,)),
             dma,
             dma,
+            pltpu.SemaphoreType.REGULAR,
+            pltpu.SemaphoreType.REGULAR,
         ],
         compiler_params=pltpu.CompilerParams(
             collective_id=0, has_side_effects=True, vmem_limit_bytes=32 * 1024 * 1024

time: 29.8 us -> 29.1 us (0.977)
  Pallas kernels: 29.1 us -> 28.4 us
    pallas_call x1, Pallas kernels: 28.3 us -> 27.6 us  [local(): pl.pallas_call(body, out_shape=(jax.ShapeDtypeStruct((WX, WY, DZ, C), BF1...]
where the time goes in v4:
time: 29.1 us; the launch traced here: 29 us
  Pallas kernels  28.4 us (98%)
  between operations  0.64 us (2%)
    pallas_call x1, Pallas kernels, local(): pl.pallas_call(body, out_shape=(jax.ShapeDtypeStruct((WX, WY, DZ, C), BF1...  27.6 us
    pallas_call x1, Pallas kernels, local(): pl.pallas_call(finish, out_shape=(jax.ShapeDtypeStruct((WX, WY, DZ, C), B...  0.79 us

profile of v4, /device:TPU:1, one launch (start us, length us, event | category | flops | bytes accessed | tf_op | source)
XLA Modules:
  0.0 29.0 jit_solution(12320791012266068973)
XLA Ops:
  0.6 27.6 %conv_backward.1 = (bf16[2,4,48,128]{3,2,1,0:T(8,128)(2,1)S(1)}, f32[2,8,128]{2,1,0:T(8,128)S(1)}) custom-call(bf16[2,4,48,128]{3,2,1,0:T(8,128)(2,1)} %inp_hbm.1, bf16[2,4,48,128]{3,2,1,0:T(8,128)(2,1)} %cot_hbm.1, bf16[27,128,128]{2,1,0:T(8,128)(2,1)} %ker_hbm.1), custom_call_target="tpu_custom_call" | custom-call | tf_op jit(solution)/shard_map/conv_backward/pallas_call | solution.py:371
  28.2 0.8 %finish.1 = (bf16[2,4,48,128]{3,2,1,0:T(8,128)(2,1)}, f32[8,8,27]{2,1,0:T(8,128)}) custom-call(bf16[2,4,48,128]{3,2,1,0:T(8,128)(2,1)S(1)} %get-tuple-element.6.ig_ref, f32[2,8,128]{2,1,0:T(8,128)S(1)} %get-tuple-element.7.sums_ref), custom_call_target="tpu_custom_call" | custom-call | tf_op jit(solution)/shard_map/finish/pallas_call | solution.py:413

commit v5 on v4

--- a/solution.py
+++ b/solution.py
@@ -17,9 +17,9 @@
 NQ = 8
 NXY = 2 * NQ
 PAIRS = 14
-ORDER = (4, 3, 5, 0, 1, 2, 6, 7, 8)
-CHUNKS = (((0, 1), (0, 1)), ((1, 3), (1, 2)), ((3, 6), (2, 4)), ((6, 9), (4, 7)))
-STEPS = ('c0', 'f0', 'y', 'c1', 'x', 'c2', 'f1', 'c3', 'f2', 'f3')
+ORDER = (4, 3, 5, 6, 7, 8, 0, 1, 2)
+CHUNKS = (((0, 1), (0, 1)), ((1, 3), (1, 2)), ((3, 5), (2, 4)), ((5, 9), (4, 7)))
+STEPS = ("c0", "f0", "y", "c1", "m", "c2", "f1", "p", "c3", "f2", "f3")
 
 
 def slot(n, jz):
@@ -34,7 +34,7 @@
 ROW = ((2, 0), (1, 0), (3, 0))
 COLUMN = ((0, 2), (0, 1), (0, 3))
 NEAR_Z = (2, 6, 1, 7)
-DIRS = tuple((dx, dy) for dx in (-1, 0, 1) for dy in (-1, 0, 1) if (dx, dy) != (0, 0))
+DIRS = tuple((dx, dy) for dx in (-1, 1, 0) for dy in (-1, 0, 1) if (dx, dy) != (0, 0))
 
 
 def blocks(w, local):
@@ -176,9 +176,9 @@
         def _():
             halo[pl.ds(*lx), pl.ds(*ly)] = jnp.zeros((lx[1], ly[1], DZ, C), BF16)
 
-    def landed(along_x):
+    def landed(along):
         for i, (dx, dy) in enumerate(DIRS):
-            if (dx != 0) != along_x:
+            if dx != along:
                 continue
 
             @pl.when(has(-dx, gx, 16) * has(-dy, gy, 16) == 1)
@@ -189,13 +189,12 @@
         jx, jy = w // 3, w % 3
         return stack[pl.ds(2 - jx, WX), pl.ds(2 - jy, WY)].reshape(VOX, 3 * C)
 
-    def sib_copy(k):
-        lo, hi = CHUNKS[k][1]
+    def sib_copy(v):
         return pltpu.make_async_remote_copy(
-            src_ref=parts.at[1 - core, pl.ds(2 * lo, 2 * (hi - lo))],
-            dst_ref=sib.at[pl.ds(2 * lo, 2 * (hi - lo))],
-            send_sem=ssend_sem.at[k],
-            recv_sem=srecv_sem.at[k],
+            src_ref=parts.at[1 - core, pl.ds(2 * v, 2)],
+            dst_ref=sib.at[pl.ds(2 * v, 2)],
+            send_sem=ssend_sem.at[v],
+            recv_sem=srecv_sem.at[v],
             device_id=(gx, other),
             device_id_type=MESH,
         )
@@ -243,16 +242,8 @@
         device_id_type=MESH,
     )
 
-    def compute(k):
-        (w_lo, w_hi), (lo, hi) = CHUNKS[k]
-        for n in range(w_lo, w_hi):
-            w = ORDER[n]
-            if RIM[w]:
-                r = product(w, RIM[w])
-                for jz in range(3):
-                    taps[slot(n, jz)] += r[:, jz * C : (jz + 1) * C]
-
-        for u in range(2 * lo, 2 * hi):
+    def turn(v):
+        for u in (2 * v, 2 * v + 1):
             for h in range(2):
                 a = jnp.concatenate(
                     [taps[2 * u, 64 * h : 64 * h + 64], taps[2 * u + 1, 64 * h : 64 * h + 64]], axis=0
@@ -260,36 +251,48 @@
                 t = a.T.reshape(NQ, 2, 8, C)
                 parts[0, u, h] = t[:, 0]
                 parts[1, u, h] = t[:, 1]
-
-        sib_copy(k).start()
+        sib_copy(v).start()
+
+    def compute(k):
+        (w_lo, w_hi), (lo, hi) = CHUNKS[k]
+        done = lo
+        for n in range(w_lo, w_hi):
+            w = ORDER[n]
+            if RIM[w]:
+                r = product(w, RIM[w])
+                for jz in range(3):
+                    taps[slot(n, jz)] += r[:, jz * C : (jz + 1) * C]
+            ready = min(hi, (slot(n, 2) + (2 if n == 0 else 1)) // 4)
+            for v in range(done, ready):
+                turn(v)
+            done = max(done, ready)
 
     def forward(k):
         lo, hi = CHUNKS[k][1]
-        sib_copy(k).wait_recv()
-
-        @pl.loop(lo, hi)
-        def _(v):
+        for v in range(lo, hi):
+            sib_copy(v).wait_recv()
             for h in range(2):
                 both = [parts[core, 2 * v + e, h] + sib[2 * v + e, h] for e in range(2)]
                 xsend[NQ * h : NQ * h + NQ, v] = jnp.concatenate(both, axis=1).astype(BF16)
-
         if k == 0:
             pl.semaphore_wait(plane_in, len(ROW))
         for d in XY:
             xy_copy(k, d).start()
+        xrecv[here, lo:hi] = xsend[here, lo:hi]
 
     for step in STEPS:
         if step == "y":
-            landed(False)
-
+            landed(0)
             for x in range(WX):
                 restack(1 + x, 0)
                 restack(1 + x, WY + 1)
-        elif step == "x":
-            landed(True)
-
+        elif step == "m":
+            landed(1)
             for y in range(WY + 2):
                 restack(0, y)
+        elif step == "p":
+            landed(-1)
+            for y in range(WY + 2):
                 restack(WX + 1, y)
         elif step[0] == "c":
             compute(int(step[1]))
@@ -311,13 +314,12 @@
         ig_ref[x] = (slope[x] * back).astype(BF16).reshape(WY, DZ, C)
 
     for k in range(len(CHUNKS)):
+        lo, hi = CHUNKS[k][1]
         xy_all(k).wait_recv()
-
-    xrecv[here] = xsend[here]
-    total = xrecv[0].astype(F32)
-    for m in range(1, NXY):
-        total = total + xrecv[m].astype(F32)
-    sums[pl.ds(0, 8 * PAIRS)] = total.reshape(8 * PAIRS, C)
+        total = xrecv[0, lo:hi].astype(F32)
+        for m in range(1, NXY):
+            total = total + xrecv[m, lo:hi].astype(F32)
+        sums[pl.ds(16 * lo, 16 * (hi - lo))] = total.reshape(16 * (hi - lo), C)
     sums[pl.ds(8 * PAIRS, C - 8 * PAIRS)] = jnp.zeros((C - 8 * PAIRS, C), F32)
     total = jnp.concatenate([sums[pl.ds(o, 16, stride=8)] for o in range(8)], axis=0)
     turned = total.T.reshape(2, NZ, 8, C)
@@ -335,8 +337,9 @@
             hop(i).wait_send()
 
     for k in range(len(CHUNKS)):
-        sib_copy(k).wait_send()
         xy_all(k).wait_send()
+    for v in range(PAIRS // 2):
+        sib_copy(v).wait_send()
 
     z_all.wait_recv()
     out = zrecv[0]
@@ -395,8 +398,8 @@
             dma((3,)),
             dma((8,)),
             dma((8,)),
-            dma((n,)),
-            dma((n,)),
+            dma((PAIRS // 2,)),
+            dma((PAIRS // 2,)),
             dma((n,)),
             dma((n,)),
             dma,

time: 29.1 us -> 28.6 us (0.983)
  Pallas kernels: 28.4 us -> 27.9 us
    pallas_call x1, Pallas kernels: 27.6 us -> 27.1 us  [local(): pl.pallas_call(body, out_shape=(jax.ShapeDtypeStruct((WX, WY, DZ, C), BF1...]
where the time goes in v5:
time: 28.6 us; the launch traced here: 28.5 us
  Pallas kernels  27.9 us (98%)
  between operations  0.64 us (2%)
    pallas_call x1, Pallas kernels, local(): pl.pallas_call(body, out_shape=(jax.ShapeDtypeStruct((WX, WY, DZ, C), BF1...  27.1 us
    pallas_call x1, Pallas kernels, local(): pl.pallas_call(finish, out_shape=(jax.ShapeDtypeStruct((WX, WY, DZ, C), B...  0.79 us

profile of v5, /device:TPU:1, one launch (start us, length us, event | category | flops | bytes accessed | tf_op | source)
XLA Modules:
  0.0 28.5 jit_solution(13431901324575669887)
XLA Ops:
  0.6 27.1 %conv_backward.1 = (bf16[2,4,48,128]{3,2,1,0:T(8,128)(2,1)S(1)}, f32[2,8,128]{2,1,0:T(8,128)S(1)}) custom-call(bf16[2,4,48,128]{3,2,1,0:T(8,128)(2,1)} %inp_hbm.1, bf16[2,4,48,128]{3,2,1,0:T(8,128)(2,1)} %cot_hbm.1, bf16[27,128,128]{2,1,0:T(8,128)(2,1)} %ker_hbm.1), custom_call_target="tpu_custom_call" | custom-call | tf_op jit(solution)/shard_map/conv_backward/pallas_call | solution.py:374
  27.7 0.8 %finish.1 = (bf16[2,4,48,128]{3,2,1,0:T(8,128)(2,1)}, f32[8,8,27]{2,1,0:T(8,128)}) custom-call(bf16[2,4,48,128]{3,2,1,0:T(8,128)(2,1)S(1)} %get-tuple-element.6.ig_ref, f32[2,8,128]{2,1,0:T(8,128)S(1)} %get-tuple-element.7.sums_ref), custom_call_target="tpu_custom_call" | custom-call | tf_op jit(solution)/shard_map/finish/pallas_call | solution.py:416

commit v6 on v5

--- a/solution.py
+++ b/solution.py
@@ -18,8 +18,9 @@
 NXY = 2 * NQ
 PAIRS = 14
 ORDER = (4, 3, 5, 6, 7, 8, 0, 1, 2)
-CHUNKS = (((0, 1), (0, 1)), ((1, 3), (1, 2)), ((3, 5), (2, 4)), ((5, 9), (4, 7)))
-STEPS = ("c0", "f0", "y", "c1", "m", "c2", "f1", "p", "c3", "f2", "f3")
+PRODUCTS = (((0, 1), (0, 1)), ((1, 3), (1, 2)), ((3, 5), (2, 4)), ((5, 7), (4, 5)), ((7, 9), (5, 7)))
+CHUNKS = ((0, 2), (2, 4), (4, 7))
+STEPS = ('c0', 'y', 'c1', 'm', 'c2', 'f0', 'p', 'c3', 'f1', 'c4', 'f2')
 
 
 def slot(n, jz):
@@ -200,7 +201,7 @@
         )
 
     def xy_copy(k, d):
-        lo, hi = CHUNKS[k][1]
+        lo, hi = CHUNKS[k]
         m, twin = xy_peer(d)
         return pltpu.make_async_remote_copy(
             src_ref=xsend.at[m, pl.ds(lo, hi - lo)],
@@ -212,7 +213,7 @@
         )
 
     def xy_all(k):
-        lo, hi = CHUNKS[k][1]
+        lo, hi = CHUNKS[k]
         return pltpu.make_async_remote_copy(
             src_ref=xsend.at[pl.ds(0, NXY - 1), pl.ds(lo, hi - lo)],
             dst_ref=xrecv.at[pl.ds(0, NXY - 1), pl.ds(lo, hi - lo)],
@@ -254,7 +255,7 @@
         sib_copy(v).start()
 
     def compute(k):
-        (w_lo, w_hi), (lo, hi) = CHUNKS[k]
+        (w_lo, w_hi), (lo, hi) = PRODUCTS[k]
         done = lo
         for n in range(w_lo, w_hi):
             w = ORDER[n]
@@ -268,7 +269,7 @@
             done = max(done, ready)
 
     def forward(k):
-        lo, hi = CHUNKS[k][1]
+        lo, hi = CHUNKS[k]
         for v in range(lo, hi):
             sib_copy(v).wait_recv()
             for h in range(2):
@@ -314,7 +315,7 @@
         ig_ref[x] = (slope[x] * back).astype(BF16).reshape(WY, DZ, C)
 
     for k in range(len(CHUNKS)):
-        lo, hi = CHUNKS[k][1]
+        lo, hi = CHUNKS[k]
         xy_all(k).wait_recv()
         total = xrecv[0, lo:hi].astype(F32)
         for m in range(1, NXY):

time: 28.6 us -> 28.7 us (level)
  no operation moved by 1% of the time
where the time goes in v6:
time: 28.7 us; the launch traced here: 28.6 us
  Pallas kernels  27.9 us (97%)
  between operations  0.64 us (2%)
    pallas_call x1, Pallas kernels, local(): pl.pallas_call(body, out_shape=(jax.ShapeDtypeStruct((WX, WY, DZ, C), BF1...  27.2 us
    pallas_call x1, Pallas kernels, local(): pl.pallas_call(finish, out_shape=(jax.ShapeDtypeStruct((WX, WY, DZ, C), B...  0.79 us

profile of v6, /device:TPU:1, one launch (start us, length us, event | category | flops | bytes accessed | tf_op | source)
XLA Modules:
  0.0 28.6 jit_solution(6456596673988025212)
XLA Ops:
  0.6 27.2 %conv_backward.1 = (bf16[2,4,48,128]{3,2,1,0:T(8,128)(2,1)S(1)}, f32[2,8,128]{2,1,0:T(8,128)S(1)}) custom-call(bf16[2,4,48,128]{3,2,1,0:T(8,128)(2,1)} %inp_hbm.1, bf16[2,4,48,128]{3,2,1,0:T(8,128)(2,1)} %cot_hbm.1, bf16[27,128,128]{2,1,0:T(8,128)(2,1)} %ker_hbm.1), custom_call_target="tpu_custom_call" | custom-call | tf_op jit(solution)/shard_map/conv_backward/pallas_call | solution.py:375
  27.8 0.8 %finish.1 = (bf16[2,4,48,128]{3,2,1,0:T(8,128)(2,1)}, f32[8,8,27]{2,1,0:T(8,128)}) custom-call(bf16[2,4,48,128]{3,2,1,0:T(8,128)(2,1)S(1)} %get-tuple-element.6.ig_ref, f32[2,8,128]{2,1,0:T(8,128)S(1)} %get-tuple-element.7.sums_ref), custom_call_target="tpu_custom_call" | custom-call | tf_op jit(solution)/shard_map/finish/pallas_call | solution.py:417

commit v7 on v6

--- a/solution.py
+++ b/solution.py
@@ -116,6 +116,27 @@
             device_id_type=MESH,
         )
 
+    load_cot.wait()
+    pl.semaphore_wait(barrier, len(DIRS) + len(ROW) + len(COLUMN) + len(NEAR_Z))
+
+    for i, (dx, dy) in enumerate(DIRS):
+        @pl.when(has(dx, gx, 16) * has(dy, gy, 16) == 1)
+        def _():
+            hop(i).start()
+
+    for d in ROW:
+        pl.semaphore_signal(plane_in, inc=1, device_id=xy_peer(d)[1], device_id_type=MESH)
+    for d in NEAR_Z:
+        pl.semaphore_signal(z_in, inc=1, device_id=z_peer((z + d) % NZ), device_id_type=MESH)
+
+
+    for i, (dx, dy) in enumerate(DIRS):
+        lx, ly = rim(dx, WX, False), rim(dy, WY, False)
+
+        @pl.when(has(-dx, gx, 16) * has(-dy, gy, 16) == 0)
+        def _():
+            halo[pl.ds(*lx), pl.ds(*ly)] = jnp.zeros((lx[1], ly[1], DZ, C), BF16)
+
     load_inp.wait()
 
     @pl.loop(0, WX)
@@ -133,7 +154,6 @@
         down = jnp.where(row == 0, 0.0, pltpu.roll(v, 1, 0))
         stack[x, y] = jnp.concatenate([up, v, down], axis=1).astype(BF16)
 
-    load_cot.wait()
 
     @pl.loop(0, WX * WY)
     def _(k):
@@ -157,26 +177,6 @@
         for jz in range(3):
             taps[slot(n, jz)] = r[:, jz * C : (jz + 1) * C]
     taps[3] = jnp.zeros((C, C), F32)
-    pl.semaphore_wait(barrier, len(DIRS) + len(ROW) + len(COLUMN) + len(NEAR_Z))
-
-    for i, (dx, dy) in enumerate(DIRS):
-        @pl.when(has(dx, gx, 16) * has(dy, gy, 16) == 1)
-        def _():
-            hop(i).start()
-
-    for d in ROW:
-        pl.semaphore_signal(plane_in, inc=1, device_id=xy_peer(d)[1], device_id_type=MESH)
-    for d in NEAR_Z:
-        pl.semaphore_signal(z_in, inc=1, device_id=z_peer((z + d) % NZ), device_id_type=MESH)
-
-
-    for i, (dx, dy) in enumerate(DIRS):
-        lx, ly = rim(dx, WX, False), rim(dy, WY, False)
-
-        @pl.when(has(-dx, gx, 16) * has(-dy, gy, 16) == 0)
-        def _():
-            halo[pl.ds(*lx), pl.ds(*ly)] = jnp.zeros((lx[1], ly[1], DZ, C), BF16)
-
     def landed(along):
         for i, (dx, dy) in enumerate(DIRS):
             if dx != along:

time: 28.7 us -> 28.7 us (level)
  no operation moved by 1% of the time
where the time goes in v7:
time: 28.7 us; the launch traced here: 28.6 us
  Pallas kernels  28 us (98%)
  between operations  0.64 us (2%)
    pallas_call x1, Pallas kernels, local(): pl.pallas_call(body, out_shape=(jax.ShapeDtypeStruct((WX, WY, DZ, C), BF1...  27.2 us
    pallas_call x1, Pallas kernels, local(): pl.pallas_call(finish, out_shape=(jax.ShapeDtypeStruct((WX, WY, DZ, C), B...  0.79 us

profile of v7, /device:TPU:1, one launch (start us, length us, event | category | flops | bytes accessed | tf_op | source)
XLA Modules:
  0.0 28.6 jit_solution(7238226895431850430)
XLA Ops:
  0.6 27.2 %conv_backward.1 = (bf16[2,4,48,128]{3,2,1,0:T(8,128)(2,1)S(1)}, f32[2,8,128]{2,1,0:T(8,128)S(1)}) custom-call(bf16[2,4,48,128]{3,2,1,0:T(8,128)(2,1)} %inp_hbm.1, bf16[2,4,48,128]{3,2,1,0:T(8,128)(2,1)} %cot_hbm.1, bf16[27,128,128]{2,1,0:T(8,128)(2,1)} %ker_hbm.1), custom_call_target="tpu_custom_call" | custom-call | tf_op jit(solution)/shard_map/conv_backward/pallas_call | solution.py:375
  27.8 0.8 %finish.1 = (bf16[2,4,48,128]{3,2,1,0:T(8,128)(2,1)}, f32[8,8,27]{2,1,0:T(8,128)}) custom-call(bf16[2,4,48,128]{3,2,1,0:T(8,128)(2,1)S(1)} %get-tuple-element.6.ig_ref, f32[2,8,128]{2,1,0:T(8,128)S(1)} %get-tuple-element.7.sums_ref), custom_call_target="tpu_custom_call" | custom-call | tf_op jit(solution)/shard_map/finish/pallas_call | solution.py:417
